TPU v7x, 32 devices: a whole 2x2x4 slice. The times are simulated.
32 devices in a mesh: band: 4 (over y, x), pair: 8 (over z, core).
Axes of the slice: x: 2, y: 2, z: 4, core: 2. Of those that a mesh axis runs over, the one named last changes fastest.
Arguments:
- visibilities: float32 [4, 16, 8, 2, 1024], P('band', 'pair'), may hold values from -6 to 6
- coherencies: bfloat16 [4, 16, 8, 2, 32, 1024], P('band', 'pair'), may hold values from -1 to 1
- block_tiles: int32 [16, 2], P('pair'), may hold values from 0 to 15, as said below
- sample_counts: int32 [16], P('pair'), may hold values from 1 to 8, as said below
- gains: float32 [4, 2, 32, 512], P('band', None, None, 'pair'), may hold values from 0.5 to 1.5
- targets: float32 [4, 2, 32, 512], P('band', None, None, 'pair'), may hold values from 0.5 to 1.5
- multipliers: float32 [4, 2, 32, 512], P('band', None, None, 'pair'), may hold values from -2 to 2
Outputs:
- new_gains: float32 [4, 2, 32, 512], P('band', None, None, 'pair')
- new_targets: float32 [4, 2, 32, 512], P('band', None, None, 'pair')
- new_multipliers: float32 [4, 2, 32, 512], P('band', None, None, 'pair')
Inputs may be any that keep to these rules, and one draw needn't show every extreme that they name: `block_tiles`: each row names two station tiles a <= b; no tile pair appears twice; the pairs (0, 15) and (15, 15) are always among them. `sample_counts`: some block has all 8 samples and some block only one.
All inputs are finite; a program needn't handle non-finite values.
Results may differ from a plain program's by a relative error of at most 0.0003.
Values sent between devices are 32-bit elements; how exact they have to be, the bound alone decides.
No kernel may reach another device: no remote copies, remote signals or barrier semaphores. Data moves between devices by JAX's collectives and lax.ppermute only.
A program may use at most 64 MiB of HBM per device.

v0:
```python
import math
import jax
import jax.numpy as jnp
from jax import lax
from jax.sharding import PartitionSpec as P

K = 32
P_SIZE = 8
TILE = 32
ITERS = 2
TIMES = 8
ridge = 0.05
penalty = 0.25


def bernstein_table(freq_count, term_count):
    positions = (jnp.arange(freq_count).astype(jnp.float32) + 0.5) / freq_count
    columns = [
        math.comb(term_count - 1, degree)
        * positions**degree
        * (1.0 - positions) ** (term_count - 1 - degree)
        for degree in range(term_count)
    ]
    return jnp.stack(columns, axis=1)


def block_terms(gains_first, gains_second, vis_block, coh_block, same_tile, valid_count):
    tile_width = gains_first.shape[-1]
    left_gains = jnp.repeat(gains_first, tile_width, axis=-1)
    right_gains = jnp.tile(gains_second, (1, 1, tile_width))
    prod_real = left_gains[0] * right_gains[0] + left_gains[1] * right_gains[1]
    prod_imag = left_gains[1] * right_gains[0] - left_gains[0] * right_gains[1]
    cohere = coh_block.astype(jnp.float32)
    coh_real = cohere[:, 0]
    coh_imag = cohere[:, 1]
    model_real = jnp.sum(prod_real[None] * coh_real - prod_imag[None] * coh_imag, axis=1)
    model_imag = jnp.sum(prod_real[None] * coh_imag + prod_imag[None] * coh_real, axis=1)
    sample_total = vis_block.shape[0]
    cell_index = jnp.arange(tile_width * tile_width)
    row_index = cell_index // tile_width
    col_index = cell_index % tile_width
    keep_cell = (row_index < col_index) | jnp.logical_not(same_tile)
    keep_time = jnp.arange(sample_total) < valid_count
    weight = (keep_time[:, None] & keep_cell[None, :]).astype(jnp.float32)
    res_real = (vis_block[:, 0] - model_real) * weight
    res_imag = (vis_block[:, 1] - model_imag) * weight
    acc_real = jnp.sum(res_real[:, None] * coh_real + res_imag[:, None] * coh_imag, axis=0)
    acc_imag = jnp.sum(res_imag[:, None] * coh_real - res_real[:, None] * coh_imag, axis=0)
    term_real = acc_real * right_gains[0] - acc_imag * right_gains[1]
    term_imag = acc_real * right_gains[1] + acc_imag * right_gains[0]
    direction_count = acc_real.shape[0]
    grad_first = (
        -jnp.stack([term_real, term_imag])
        .reshape(2, direction_count, tile_width, tile_width)
        .sum(axis=3)
    )
    other_real = acc_real * left_gains[0] + acc_imag * left_gains[1]
    other_imag = acc_real * left_gains[1] - acc_imag * left_gains[0]
    grad_second = (
        -jnp.stack([other_real, other_imag])
        .reshape(2, direction_count, tile_width, tile_width)
        .sum(axis=2)
    )
    return (grad_first, grad_second)


def data_gradient(gain_band, vis_band, coh_band, block_tiles, sample_counts):
    direction_count = gain_band.shape[1]
    station_count = gain_band.shape[2]
    tile_count = station_count // TILE
    tile_range = jnp.arange(tile_count)
    onehot_first = (block_tiles[:, 0:1] == tile_range[None, :]).astype(jnp.float32)
    onehot_second = (block_tiles[:, 1:2] == tile_range[None, :]).astype(jnp.float32)
    grid = gain_band.reshape(2, direction_count, tile_count, TILE)
    tiles_first = jnp.einsum("bn,cknt->bckt", onehot_first, grid, precision=lax.Precision.HIGHEST)
    tiles_second = jnp.einsum("bn,cknt->bckt", onehot_second, grid, precision=lax.Precision.HIGHEST)
    same_tile = block_tiles[:, 0] == block_tiles[:, 1]
    grad_first, grad_second = jax.vmap(block_terms)(
        tiles_first, tiles_second, vis_band, coh_band, same_tile, sample_counts
    )
    total = jnp.einsum("bn,bckt->cknt", onehot_first, grad_first, precision=lax.Precision.HIGHEST)
    total = total + jnp.einsum(
        "bn,bckt->cknt", onehot_second, grad_second, precision=lax.Precision.HIGHEST
    )
    return total.reshape(2, direction_count, station_count)


def local(visibilities, coherencies, block_tiles, sample_counts, gains, targets, multipliers):
    pair_count = lax.axis_size("pair")
    band_count = lax.axis_size("band")
    station_local = gains.shape[3]
    block_total = block_tiles.shape[0] * pair_count
    tile_count = station_local * pair_count // TILE
    step_size = 0.25 * tile_count * K / (TIMES * TILE * block_total)
    current = gains
    for iteration in range(ITERS):
        whole_gains = lax.all_gather(current, "pair", axis=3, tiled=True)
        partial_value = jax.vmap(data_gradient, in_axes=(0, 0, 0, None, None))(
            whole_gains, visibilities, coherencies, block_tiles, sample_counts
        )
        summed = lax.psum_scatter(partial_value, "pair", scatter_dimension=3, tiled=True)
        current = current - step_size * summed - penalty * (current - targets + multipliers)
    freq_local = gains.shape[0]
    freq_total = freq_local * band_count
    basis_table = bernstein_table(freq_total, P_SIZE)
    normal = jnp.dot(basis_table.T, basis_table, precision=lax.Precision.HIGHEST) + ridge * jnp.eye(
        P_SIZE, dtype=jnp.float32
    )
    factor = jnp.linalg.cholesky(normal)
    flattened = (current + multipliers).reshape(freq_local, -1)
    own_basis = lax.dynamic_slice_in_dim(
        basis_table, lax.axis_index("band") * freq_local, freq_local, 0
    )
    all_bands = lax.all_gather(flattened, "band", axis=0, tiled=True)
    moments = jnp.dot(basis_table.T, all_bands, precision=lax.Precision.HIGHEST)
    coeffs = jax.scipy.linalg.cho_solve((factor, True), moments)
    fitted = jnp.dot(own_basis, coeffs, precision=lax.Precision.HIGHEST).reshape(current.shape)
    return (current, fitted, multipliers + current - fitted)


def solution(mesh):
    placed = (
        P("band", "pair", None, None, None),
        P("band", "pair", None, None, None, None),
        P("pair", None),
        P("pair"),
        P("band", None, None, "pair"),
        P("band", None, None, "pair"),
        P("band", None, None, "pair"),
    )
    return jax.shard_map(
        local,
        mesh=mesh,
        in_specs=placed,
        out_specs=(
            P("band", None, None, "pair"),
            P("band", None, None, "pair"),
            P("band", None, None, "pair"),
        ),
        check_vma=False,
    )
```

profile of v0, /device:TPU:0, one launch (start us, length us, event | category | flops | bytes accessed | tf_op | source)
XLA Modules:
  0.0 149.3 jit_solution(11101035761976110209)
XLA Ops:
  7.2 1.0 slice_reduce_fusion.1
  8.2 0.9 not_reduce_fusion
  9.1 0.9 copy.27
  10.0 16.5 %all_gather.9 = f32[1,2,32,512]{2,1,0,3:T(2,128)S(1)} all-gather(f32[1,2,32,64]{2,1,0,3:T(2,128)S(1)} %copy.27), channel_id=1, replica_groups=mesh['band'=4,'pair'=8] {'pair'}, dimensions={3}, use_global_device_ids=true | all-gather | bytes 147456 | tf_op jit(solution)/shard_map/all_gather | solution.py:97
  27.7 1.0 broadcast_in_dim.10
  29.2 1.0 tile.9
  30.1 2.1 %convert_element_type.71 = f32[1,2,8,2,32,1024]{5,4,3,2,1,0:T(8,128)S(1)} convert(bf16[1,2,8,2,32,1024]{5,4,3,2,1,0:T(8,128)(2,1)} %param.8) | non-fusion elementwise | flops 1048576 | bytes 6291456 | tf_op jit(solution)/shard_map/vmap(vmap())/convert_element_type | solution.py:33
  32.6 0.8 subtract_reduce_fusion.3
  35.1 0.7 reshape.953
  36.9 0.7 reshape.954
  38.9 1.0 reshape.971
  40.4 0.7 cholesky.16
  41.2 30.8 %reduce-scatter.7.cloned.1.call-done = f32[64,64]{1,0:T(8,128)} async-done(((f32[512,64]{1,0:T(8,128)}), f32[64,64]{1,0:T(8,128)}) %reduce-scatter.7.cloned.1.call-update) | async-done | bytes 16400
  72.0 0.9 reshape.972
  73.1 15.1 %all_gather.10 = f32[1,2,32,512]{2,1,0,3:T(2,128)S(1)} all-gather(f32[1,2,32,64]{2,1,0,3:T(2,128)S(1)} %copy.35), channel_id=1, replica_groups=mesh['band'=4,'pair'=8] {'pair'}, dimensions={3}, use_global_device_ids=true | all-gather | bytes 147456 | tf_op jit(solution)/shard_map/all_gather | solution.py:97
  89.7 1.0 broadcast_in_dim.12
  90.9 1.0 tile.21
  91.9 3.2 %subtract_reduce_fusion.1 = (f32[2,8,1024]{2,1,0:T(8,128)S(1)}, f32[2,8,1024]{2,1,0:T(8,128)S(1)}) fusion(f32[1,2,8,2,32,1024]{5,4,3,2,1,0:T(8,128)} %copy-done, f32[2,32,1024]{2,1,0:T(8,128)S(1)} %get-tuple-element.20, f32[2,32,1024]{2,1,0:T(8,128)S(1)} %get-tuple-element.19), kind=kLoop, calls=%fused_computation.5 | loop fusion | flops 4161536 | bytes 4849664 | tf_op jit(solution)/shard_map/vmap(vmap())/reduce_sum | solution.py:36
  96.2 0.7 reshape.958
  97.4 0.7 reshape.957
  100.0 1.0 reshape.973
  103.0 27.3 %reduce-scatter.9.cloned.1.call-done = f32[64,64]{1,0:T(8,128)} async-done(((f32[512,64]{1,0:T(8,128)}), f32[64,64]{1,0:T(8,128)}) %reduce-scatter.9.cloned.1.call-update) | async-done | bytes 16400
  130.2 0.9 reshape.974
  131.9 8.2 %all-gather = f32[4,1,4096]{2,1,0:T(1,128)S(1)} all-gather(f32[1,1,4096]{2,1,0:T(1,128)S(1)} %reshape.962), channel_id=1, replica_groups=mesh['band'=4,'pair'=8] {'band'}, dimensions={0}, use_global_device_ids=true | all-gather | bytes 81920 | tf_op jit(solution)/shard_map/all_gather | solution.py:114
  (87 shorter events, 17.1 us)
Async XLA Ops:
  7.2 64.8 %reduce-scatter.7.cloned.1.call-start = ((), (), s32[]{:S(2)}) async-start(), calls=%async_computation.2 | async-start | bytes 294912
  30.1 2.1 %copy-start.4 = (f32[1,2,8,2,1024]{4,3,2,1,0:T(2,128)S(1)}, f32[1,2,8,2,1024]{4,3,2,1,0:T(2,128)}, u32[]{:S(2)}) copy-start(f32[1,2,8,2,1024]{4,3,2,1,0:T(2,128)} %param.7) | copy-start | bytes 393220
  30.1 2.2 %copy-start.7 = (s32[2]{0:T(128)S(1)}, s32[2]{0:T(128)}, u32[]{:S(2)}) copy-start(s32[2]{0:T(128)} %param.10) | copy-start | bytes 28
  32.2 1.9 %copy-start = (f32[1,2,8,2,32,1024]{5,4,3,2,1,0:T(8,128)}, f32[1,2,8,2,32,1024]{5,4,3,2,1,0:T(8,128)S(1)}, u32[]{:S(2)}) copy-start(f32[1,2,8,2,32,1024]{5,4,3,2,1,0:T(8,128)S(1)} %convert_element_type.71) | copy-start | bytes 12582916
  38.0 34.9 %copy-start.2 = (f32[1,2,32,64]{3,2,1,0:T(8,128)S(1)}, f32[1,2,32,64]{3,2,1,0:T(8,128)}, u32[]{:S(2)}) copy-start(f32[1,2,32,64]{3,2,1,0:T(8,128)} %param.11) | copy-start | bytes 49156
  38.1 34.9 %copy-start.5 = (f32[1,2,32,64]{3,2,1,0:T(8,128)S(1)}, f32[1,2,32,64]{3,2,1,0:T(8,128)}, u32[]{:S(2)}) copy-start(f32[1,2,32,64]{3,2,1,0:T(8,128)} %param.13) | copy-start | bytes 49156
  38.1 34.9 %copy-start.6 = (f32[1,2,32,64]{3,2,1,0:T(8,128)S(1)}, f32[1,2,32,64]{3,2,1,0:T(8,128)}, u32[]{:S(2)}) copy-start(f32[1,2,32,64]{3,2,1,0:T(8,128)} %param.12) | copy-start | bytes 49156
  39.9 90.3 %reduce-scatter.9.cloned.1.call-start = ((), (), s32[]{:S(2)}) async-start(), calls=%async_computation.3 | async-start | bytes 294912
  91.9 3.5 %copy-start.1 = (f32[1,2,8,2,32,1024]{5,4,3,2,1,0:T(8,128)S(1)}, f32[1,2,8,2,32,1024]{5,4,3,2,1,0:T(8,128)}, u32[]{:S(2)}) copy-start(f32[1,2,8,2,32,1024]{5,4,3,2,1,0:T(8,128)} %copy-done) | copy-start | bytes 12582916
  141.8 0.6 copy-start.3
Sparse Core Ops, SparseCore 0:
  40.1 31.8 reduce-scatter.6
  101.2 29.0 reduce-scatter.8
where the time goes:
time: 150 us; the launch traced here: 149 us
  waiting for transfers between devices  58.1 us (39%)
  blocking collectives  39.9 us (27%)
  local copies, waits for them, and re-layouts  16.4 us (11%)
  other arithmetic  15.4 us (10%)
  between operations  14.5 us (10%)
  matrix products  4.94 us (3%)
    unnamed x4, waiting for transfers between devices  58.1 us
    all_gather x2, blocking collectives, local(): whole_gains = lax.all_gather(current, 'pair', axis=3, tiled=True)  31.6 us
    all_gather x1, blocking collectives, local(): all_bands = lax.all_gather(flattened, 'band', axis=0, tiled=True)  8.23 us
    unnamed x26, local copies, waits for them, and re-layouts  6.34 us
    reduce_sum x2, other arithmetic, block_terms(): jnp.sum(prod_real[None] * coh_real - prod_imag[None] * coh_imag, axis=1)  3.97 us
    broadcast_in_dim x4, local copies, waits for them, and re-layouts, block_terms(): left_gains = jnp.repeat(gains_first, tile_width, axis=-1)  3.11 us
  transfers between devices with their start and end apart: 2, of which 2 were waited for; matrix products, arithmetic and copies ran while one was open for 2% of the time, Pallas kernels for 0%

commit v1 on v0

--- a/solution.py
+++ b/solution.py
@@ -3,6 +3,7 @@
 import jax.numpy as jnp
 from jax import lax
 from jax.sharding import PartitionSpec as P
+from jax.lax import axis_index, axis_size, ppermute
 
 K = 32
 P_SIZE = 8
@@ -11,6 +12,21 @@
 TIMES = 8
 ridge = 0.05
 penalty = 0.25
+
+
+def frames_update(x_part, on_dim):
+    val2 = axis_size("pair")
+    top = axis_index("pair")
+    heard, o_now = (val2, top)
+    long_array, lower = (x_part, 1)
+    while lower < heard:
+        step_out = tuple(((nth, nth ^ lower) for nth in range(heard)))
+        then = ppermute(long_array, axis_name="pair", perm=step_out)
+        v_now = jnp.concatenate([long_array, then], on_dim)
+        local_now = jnp.concatenate([then, long_array], on_dim)
+        long_array = jnp.where(o_now & lower == 0, v_now, local_now)
+        lower = 2 * lower
+    return long_array
 
 
 def bernstein_table(freq_count, term_count):
@@ -94,7 +110,7 @@
     step_size = 0.25 * tile_count * K / (TIMES * TILE * block_total)
     current = gains
     for iteration in range(ITERS):
-        whole_gains = lax.all_gather(current, "pair", axis=3, tiled=True)
+        whole_gains = frames_update(current, on_dim=3)
         partial_value = jax.vmap(data_gradient, in_axes=(0, 0, 0, None, None))(
             whole_gains, visibilities, coherencies, block_tiles, sample_counts
         )

time: 150 us -> 147 us (0.980)
  blocking collectives: 39.9 us -> 8.28 us
  waiting for transfers between devices: 58.1 us -> 72.9 us
  starting transfers between devices: 0.08 us -> 6.63 us
  other arithmetic: 15.4 us -> 21.9 us
    all_gather x2 -> x0, blocking collectives: 31.6 us -> none  [local(): whole_gains = lax.all_gather(current, 'pair', axis=3, tiled=True)]
    ppermute x0 -> x6, waiting for transfers between devices: none -> 13.8 us  [frames_update(): then = ppermute(long_array, axis_name='pair', perm=step_out)]
    ppermute x0 -> x6, starting transfers between devices: none -> 6.37 us  [frames_update(): then = ppermute(long_array, axis_name='pair', perm=step_out)]
    reduce_sum x2, other arithmetic: 3.97 us -> 6.35 us  [block_terms(): jnp.sum(prod_real[None] * coh_real - prod_imag[None] * coh_imag, axis=1)]
    convert_element_type x1, other arithmetic: 2.07 us -> 4.01 us  [block_terms(): cohere = coh_block.astype(jnp.float32)]
    concatenate x0 -> x8, local copies, waits for them, and re-layouts: none -> 1.58 us  [frames_update(): v_now = jnp.concatenate([long_array, then], on_dim)]
    unnamed x26 -> x23, local copies, waits for them, and re-layouts: 6.34 us -> 4.99 us
  transfers between devices with their start and end apart: 2 -> 8, of which waited for: 2 -> 7; matrix products, arithmetic and copies ran while one was open for 2% -> 9% of each run, Pallas kernels for 0% -> 0%
where the time goes in v1:
time: 147 us; the launch traced here: 146 us
  waiting for transfers between devices  72.9 us (50%)
  other arithmetic  21.9 us (15%)
  local copies, waits for them, and re-layouts  16.9 us (11%)
  between operations  14.6 us (10%)
  blocking collectives  8.28 us (6%)
  starting transfers between devices  6.63 us (5%)
  matrix products  5.03 us (3%)
    unnamed x4, waiting for transfers between devices  59.2 us
    ppermute x6, waiting for transfers between devices, frames_update(): then = ppermute(long_array, axis_name='pair', perm=step_out)  13.8 us
    all_gather x1, blocking collectives, local(): all_bands = lax.all_gather(flattened, 'band', axis=0, tiled=True)  8.28 us
    ppermute x6, starting transfers between devices, frames_update(): then = ppermute(long_array, axis_name='pair', perm=step_out)  6.37 us
    reduce_sum x2, other arithmetic, block_terms(): jnp.sum(prod_real[None] * coh_real - prod_imag[None] * coh_imag, axis=1)  6.35 us
    unnamed x23, local copies, waits for them, and re-layouts  4.99 us
    convert_element_type x1, other arithmetic, block_terms(): cohere = coh_block.astype(jnp.float32)  4.01 us
    broadcast_in_dim x4, local copies, waits for them, and re-layouts, block_terms(): left_gains = jnp.repeat(gains_first, tile_width, axis=-1)  3.11 us
  transfers between devices with their start and end apart: 8, of which 7 were waited for; matrix products, arithmetic and copies ran while one was open for 9% of the time, Pallas kernels for 0%

profile of v1, /device:TPU:0, one launch (start us, length us, event | category | flops | bytes accessed | tf_op | source)
XLA Modules:
  0.0 146.3 jit_solution(4256167113373198162)
XLA Ops:
  7.8 1.0 slice_reduce_fusion.1
  8.7 0.9 not_reduce_fusion
  9.7 1.1 fusion.91
  11.6 0.9 concatenate.232
  12.5 4.0 %convert_element_type.71 = f32[1,2,8,2,32,1024]{5,4,3,2,1,0:T(8,128)} convert(bf16[1,2,8,2,32,1024]{5,4,3,2,1,0:T(8,128)(2,1)} %param.8) | non-fusion elementwise | flops 1048576 | bytes 6291456 | tf_op jit(solution)/shard_map/vmap(vmap())/convert_element_type | solution.py:49
  16.7 2.6 %collective-permute-start.1 = (f32[1,2,32,128]{3,2,1,0:T(8,128)S(1)}, f32[1,2,32,128]{3,2,1,0:T(8,128)S(1)}, u32[]{:S(2)}, u32[]{:S(2)}) collective-permute-start(f32[1,2,32,128]{3,2,1,0:T(8,128)S(1)} %maximum_select_fusion.12), channel_id=1, source_target_pairs={{0,2},{1,3},{2,0},{3,1},{4,6},{5,7},{6,4},{7,5},{8,10},{9,11},{10,... | collective-permute-start | bytes 98312 | tf_op jit(solution)/shard_map/ppermute | solution.py:24
  19.7 1.7 %collective-permute-done.1 = f32[1,2,32,128]{3,2,1,0:T(8,128)S(1)} collective-permute-done((f32[1,2,32,128]{3,2,1,0:T(8,128)S(1)}, f32[1,2,32,128]{3,2,1,0:T(8,128)S(1)}, u32[]{:S(2)}, u32[]{:S(2)}) %collective-permute-start.1) | collective-permute-done | bytes 32800 | tf_op jit(solution)/shard_map/ppermute | solution.py:24
  21.4 3.0 %collective-permute-start.2 = (f32[1,2,32,256]{3,2,1,0:T(8,128)S(1)}, f32[1,2,32,256]{3,2,1,0:T(8,128)S(1)}, u32[]{:S(2)}, u32[]{:S(2)}) collective-permute-start(f32[1,2,32,256]{3,2,1,0:T(8,128)S(1)} %maximum_select_fusion.10), channel_id=1, source_target_pairs={{0,4},{1,5},{2,6},{3,7},{4,0},{5,1},{6,2},{7,3},{8,12},{9,13},{10,... | collective-permute-start | bytes 196616 | tf_op jit(solution)/shard_map/ppermute | solution.py:24
  24.7 2.4 %collective-permute-done.2 = f32[1,2,32,256]{3,2,1,0:T(8,128)S(1)} collective-permute-done((f32[1,2,32,256]{3,2,1,0:T(8,128)S(1)}, f32[1,2,32,256]{3,2,1,0:T(8,128)S(1)}, u32[]{:S(2)}, u32[]{:S(2)}) %collective-permute-start.2) | collective-permute-done | bytes 65568 | tf_op jit(solution)/shard_map/ppermute | solution.py:24
  28.1 1.0 broadcast_in_dim.10
  29.6 1.0 tile.9
  30.6 3.2 %subtract_reduce_fusion.3 = (f32[2,8,1024]{2,1,0:T(8,128)S(1)}, f32[2,8,1024]{2,1,0:T(8,128)S(1)}) fusion(f32[1,2,8,2,32,1024]{5,4,3,2,1,0:T(8,128)} %convert_element_type.71, f32[2,32,1024]{2,1,0:T(8,128)S(1)} %get-tuple-element.26, f32[2,32,1024]{2,1,0:T(8,128)S(1)} %get-tuple-element.25), kind=kLoop, calls=%fused_computation.9 | loop fusion | flops 4161536 | bytes 4849664 | tf_op jit(solution)/shard_map/vmap(vmap())/reduce_sum | solution.py:52
  38.8 1.0 reshape.1423
  41.0 31.5 %reduce-scatter.7.cloned.1.call-done = f32[64,64]{1,0:T(8,128)} async-done(((f32[512,64]{1,0:T(8,128)}), f32[64,64]{1,0:T(8,128)}) %reduce-scatter.7.cloned.1.call-update) | async-done | bytes 16400
  73.7 1.1 collective-permute-done.3
  75.2 3.6 %collective-permute-done.4 = f32[1,2,32,128]{3,2,1,0:T(8,128)S(1)} collective-permute-done((f32[1,2,32,128]{3,2,1,0:T(8,128)S(1)}, f32[1,2,32,128]{3,2,1,0:T(8,128)S(1)}, u32[]{:S(2)}, u32[]{:S(2)}) %collective-permute-start.4) | collective-permute-done | bytes 32800 | tf_op jit(solution)/shard_map/ppermute | solution.py:24
  79.2 5.0 %collective-permute-done.5 = f32[1,2,32,256]{3,2,1,0:T(8,128)S(1)} collective-permute-done((f32[1,2,32,256]{3,2,1,0:T(8,128)S(1)}, f32[1,2,32,256]{3,2,1,0:T(8,128)S(1)}, u32[]{:S(2)}, u32[]{:S(2)}) %collective-permute-start.5) | collective-permute-done | bytes 65568 | tf_op jit(solution)/shard_map/ppermute | solution.py:24
  85.6 1.0 broadcast_in_dim.12
  86.7 1.0 tile.21
  87.8 3.2 %subtract_reduce_fusion.1 = (f32[2,8,1024]{2,1,0:T(8,128)S(1)}, f32[2,8,1024]{2,1,0:T(8,128)S(1)}) fusion(f32[1,2,8,2,32,1024]{5,4,3,2,1,0:T(8,128)} %convert_element_type.71, f32[2,32,1024]{2,1,0:T(8,128)S(1)} %get-tuple-element.20, f32[2,32,1024]{2,1,0:T(8,128)S(1)} %get-tuple-element.19), kind=kLoop, calls=%fused_computation.5 | loop fusion | flops 4161536 | bytes 4849664 | tf_op jit(solution)/shard_map/vmap(vmap())/reduce_sum | solution.py:52
  91.9 0.9 fusion.6
  96.6 1.0 reshape.1425
  99.6 27.7 %reduce-scatter.9.cloned.1.call-done = f32[64,64]{1,0:T(8,128)} async-done(((f32[512,64]{1,0:T(8,128)}), f32[64,64]{1,0:T(8,128)}) %reduce-scatter.9.cloned.1.call-update) | async-done | bytes 16400
  128.9 8.3 %all-gather = f32[4,1,4096]{2,1,0:T(1,128)S(1)} all-gather(f32[1,1,4096]{2,1,0:T(1,128)S(1)} %reshape.1414), channel_id=1, replica_groups=mesh['band'=4,'pair'=8] {'band'}, dimensions={0}, use_global_device_ids=true | all-gather | bytes 81920 | tf_op jit(solution)/shard_map/all_gather | solution.py:130
  (109 shorter events, 24.0 us)
Async XLA Ops:
  7.2 65.3 %reduce-scatter.7.cloned.1.call-start = ((), (), s32[]{:S(2)}) async-start(), calls=%async_computation.2 | async-start | bytes 294912
  7.2 9.4 %collective-permute-start = (f32[1,2,32,64]{3,2,1,0:T(8,128)}, f32[1,2,32,64]{3,2,1,0:T(8,128)S(1)}, u32[]{:S(2)}, u32[]{:S(2)}) collective-permute-start(f32[1,2,32,64]{3,2,1,0:T(8,128)} %param.11), channel_id=1, source_target_pairs={{0,1},{1,0},{2,3},{3,2},{4,5},{5,4},{6,7},{7,6},{8,9},{9,8},{10,11... | collective-permute-start | bytes 49160 | tf_op jit(solution)/shard_map/ppermute | solution.py:24
  12.5 4.1 %copy-start.3 = (f32[1,2,32,64]{3,2,1,0:T(8,128)S(1)}, f32[1,2,32,64]{3,2,1,0:T(8,128)}, u32[]{:S(2)}) copy-start(f32[1,2,32,64]{3,2,1,0:T(8,128)} %param.11) | copy-start | bytes 49156
  16.7 4.7 %collective-permute-start.1 = (f32[1,2,32,128]{3,2,1,0:T(8,128)S(1)}, f32[1,2,32,128]{3,2,1,0:T(8,128)S(1)}, u32[]{:S(2)}, u32[]{:S(2)}) collective-permute-start(f32[1,2,32,128]{3,2,1,0:T(8,128)S(1)} %maximum_select_fusion.12), channel_id=1, source_target_pairs={{0,2},{1,3},{2,0},{3,1},{4,6},{5,7},{6,4},{7,5},{8,10},{9,11},{10,... | collective-permute-start | bytes 98312 | tf_op jit(solution)/shard_map/ppermute | solution.py:24
  21.4 5.6 %collective-permute-start.2 = (f32[1,2,32,256]{3,2,1,0:T(8,128)S(1)}, f32[1,2,32,256]{3,2,1,0:T(8,128)S(1)}, u32[]{:S(2)}, u32[]{:S(2)}) collective-permute-start(f32[1,2,32,256]{3,2,1,0:T(8,128)S(1)} %maximum_select_fusion.10), channel_id=1, source_target_pairs={{0,4},{1,5},{2,6},{3,7},{4,0},{5,1},{6,2},{7,3},{8,12},{9,13},{10,... | collective-permute-start | bytes 196616 | tf_op jit(solution)/shard_map/ppermute | solution.py:24
  30.6 3.5 %copy-start = (f32[1,2,8,2,32,1024]{5,4,3,2,1,0:T(8,128)S(1)}, f32[1,2,8,2,32,1024]{5,4,3,2,1,0:T(8,128)}, u32[]{:S(2)}) copy-start(f32[1,2,8,2,32,1024]{5,4,3,2,1,0:T(8,128)} %convert_element_type.71) | copy-start | bytes 12582916
  37.9 35.5 %copy-start.5 = (f32[1,2,32,64]{3,2,1,0:T(8,128)S(1)}, f32[1,2,32,64]{3,2,1,0:T(8,128)}, u32[]{:S(2)}) copy-start(f32[1,2,32,64]{3,2,1,0:T(8,128)} %param.13) | copy-start | bytes 49156
  38.0 35.5 %copy-start.6 = (f32[1,2,32,64]{3,2,1,0:T(8,128)S(1)}, f32[1,2,32,64]{3,2,1,0:T(8,128)}, u32[]{:S(2)}) copy-start(f32[1,2,32,64]{3,2,1,0:T(8,128)} %param.12) | copy-start | bytes 49156
  39.8 87.4 %reduce-scatter.9.cloned.1.call-start = ((), (), s32[]{:S(2)}) async-start(), calls=%async_computation.3 | async-start | bytes 294912
  73.5 1.3 collective-permute-start.3
  74.8 4.0 %collective-permute-start.4 = (f32[1,2,32,128]{3,2,1,0:T(8,128)S(1)}, f32[1,2,32,128]{3,2,1,0:T(8,128)S(1)}, u32[]{:S(2)}, u32[]{:S(2)}) collective-permute-start(f32[1,2,32,128]{3,2,1,0:T(8,128)S(1)} %maximum_select_fusion.14), channel_id=1, source_target_pairs={{0,2},{1,3},{2,0},{3,1},{4,6},{5,7},{6,4},{7,5},{8,10},{9,11},{10,... | collective-permute-start | bytes 98312 | tf_op jit(solution)/shard_map/ppermute | solution.py:24
  78.8 5.4 %collective-permute-start.5 = (f32[1,2,32,256]{3,2,1,0:T(8,128)S(1)}, f32[1,2,32,256]{3,2,1,0:T(8,128)S(1)}, u32[]{:S(2)}, u32[]{:S(2)}) collective-permute-start(f32[1,2,32,256]{3,2,1,0:T(8,128)S(1)} %maximum_select_fusion.11), channel_id=1, source_target_pairs={{0,4},{1,5},{2,6},{3,7},{4,0},{5,1},{6,2},{7,3},{8,12},{9,13},{10,... | collective-permute-start | bytes 196616 | tf_op jit(solution)/shard_map/ppermute | solution.py:24
  87.8 3.5 %copy-start.1 = (f32[1,2,8,2,32,1024]{5,4,3,2,1,0:T(8,128)S(1)}, f32[1,2,8,2,32,1024]{5,4,3,2,1,0:T(8,128)}, u32[]{:S(2)}) copy-start(f32[1,2,8,2,32,1024]{5,4,3,2,1,0:T(8,128)} %convert_element_type.71) | copy-start | bytes 12582916
  92.8 1.2 copy-start.2
  138.8 0.6 copy-start.4
Sparse Core Ops, SparseCore 0:
  40.0 32.4 reduce-scatter.6
  97.8 29.4 reduce-scatter.8
